TPU v7x, 32 devices: a whole 2x2x4 slice. The times are simulated.
32 devices in a mesh: dp: 8 (over y, x, core), expert: 4 (over z).
Axes of the slice: x: 2, y: 2, z: 4, core: 2. Of those that a mesh axis runs over, the one named last changes fastest.
Arguments:
- tokens: bfloat16 [8192, 2048], P(('dp', 'expert')), may hold values from -6 to 6
- cotangent: bfloat16 [8192, 2048], P(('dp', 'expert')), may hold values from -6 to 6
- routes: int32 [8192, 2], P(('dp', 'expert')), may hold values from 0 to 3, all different within a row; in each aligned block of 256 rows (0 to 255, 256 to 511, ...) at most 192 rows name the same one
- gate_probs: float32 [8192, 2], P(('dp', 'expert')), may hold values from 0.2 to 1
- w_up: bfloat16 [4, 2048, 768], P('expert'), may hold values from -0.125 to 0.125
- w_down: bfloat16 [4, 768, 2048], P('expert'), may hold values from -0.21875 to 0.21875
- decay_rate: float32 [4, 768], P('expert'), may hold values from 0.3 to 0.95
Outputs:
- layer_out: bfloat16 [8192, 2048], P(('dp', 'expert'))
- token_grad: bfloat16 [8192, 2048], P(('dp', 'expert'))
- gate_grad: float32 [8192, 2], P(('dp', 'expert'))
- up_grad: float32 [4, 2048, 768], P('expert', 'dp')
- down_grad: float32 [4, 768, 2048], P('expert', None, 'dp')
Inputs may be any that keep to these rules, and one draw needn't show every extreme that they name: `routes`: each token names two different experts; among the 256 rows of one device no expert is named by more than 192 rows, and in every draw some expert is named by exactly 192 rows of some device.
All inputs are finite; a program needn't handle non-finite values.
Results may differ from a plain program's by a relative error of at most 0.015.
Values may be sent and summed in bfloat16 or wider, within the bound.
A program may use at most 128 MiB of HBM per device.

v0:
```python
from functools import partial

import jax
import jax.numpy as jnp
from jax import lax
from jax.experimental import pallas as pl
from jax.experimental.pallas import tpu as pltpu
from jax.sharding import PartitionSpec as P

STEPS = 4
SHARP = 4.0

BF = jnp.bfloat16
F32 = jnp.float32


def rate_and_slope(current, decay):
    v = jnp.zeros_like(current)
    dv = jnp.zeros_like(current)
    total = jnp.zeros_like(current)
    slope = jnp.zeros_like(current)
    for _ in range(STEPS):
        v = decay * v + current
        dv = decay * dv + 1.0
        s = jax.nn.sigmoid(SHARP * (v - 1.0))
        ds = SHARP * s * (1.0 - s) * dv
        v = v - s
        dv = dv - ds
        total = total + s
        slope = slope + ds
    return total / STEPS, slope / STEPS


def mm(a, b, dims):
    return lax.dot_general(a, b, (dims, ((), ())), preferred_element_type=F32)


def expert_block(x, cot, gate, w_up, w_down, decay):
    rates, slope = rate_and_slope(mm(x, w_up, ((1,), (0,))), decay)
    rates = rates.astype(BF)
    cot32 = cot.astype(F32)
    scaled = (gate[:, None] * cot32).astype(BF)
    out = mm(rates, w_down, ((1,), (0,))).astype(BF).astype(F32)
    layer = gate[:, None] * out
    dots = jnp.sum(cot32 * out, axis=1)
    rate_grad = mm(scaled, w_down, ((1,), (1,)))
    current_grad = (rate_grad * slope).astype(BF)
    back = mm(current_grad, w_up, ((1,), (1,))).astype(BF).astype(F32)
    return layer, dots, back, rates, scaled, current_grad


def flip(pos, mask):
    for k in range(mask.bit_length()):
        b = 1 << k
        if mask & b:
            pos = pos + b * (1 - 2 * ((pos // b) % 2))
    return pos


def bit_orders(parts):
    bits = [1 << k for k in range(parts.bit_length() - 1)]
    rest = bits[1:]
    cut = len(rest) // 2
    return bits[:1] + rest[:cut] + rest[cut:], bits[:1] + rest[cut:] + rest[:cut]


def greet(n, parts):
    ex, dp = lax.axis_index("expert"), lax.axis_index("dp")
    barrier = pltpu.get_barrier_semaphore()
    masks = list(range(1, n // 2 + 1))
    for d in masks:
        pl.semaphore_signal(barrier, inc=1, device_id={"expert": flip(ex, d)}, device_id_type=pl.DeviceIdType.MESH)
    bits = bit_orders(parts)[0]
    for b in bits:
        pl.semaphore_signal(barrier, inc=1, device_id={"dp": flip(dp, b)}, device_id_type=pl.DeviceIdType.MESH)
    pl.semaphore_wait(barrier, len(masks) + len(bits))
    return ex, dp


class Sender:
    def __init__(self, send, recv):
        self.send, self.recv, self.count, self.all = send, recv, 0, []

    def start(self, src, dst, axis, target):
        k = self.count
        self.count += 1
        copy = pltpu.make_async_remote_copy(
            src_ref=src, dst_ref=dst, send_sem=self.send.at[k], recv_sem=self.recv.at[k],
            device_id={axis: target}, device_id_type=pl.DeviceIdType.MESH,
        )
        copy.start()
        self.all.append(copy)
        return copy

    def drain(self):
        for copy in self.all:
            copy.wait_send()


def dispatch_kernel(n, parts, x, c, t, up, down, dec, xo, co, to, upo, downo, deco, send, recv):
    ex, dp = greet(n, parts)
    half = n // 2
    s = Sender(send, recv)
    mate = flip(ex, half)
    first_up = s.start(up.at[dp], upo.at[dp], "expert", mate)
    first_down = s.start(down.at[dp], downo.at[dp], "expert", mate)
    late = [s.start(dec, deco, "expert", mate)]
    for d in range(1, half):
        to_dev = flip(ex, d)
        late.append(s.start(t, to.at[d - 1], "expert", to_dev))
        late.append(s.start(x, xo.at[d - 1], "expert", to_dev))
        late.append(s.start(c, co.at[d - 1], "expert", to_dev))
    orders = [o[::-1] for o in bit_orders(parts)]
    waiting = [[first_up], [first_down]]
    held = [[0], [0]]
    for stage in range(len(orders[0])):
        for a, buf in ((0, upo), (1, downo)):
            for copy in waiting[a]:
                copy.wait_recv()
            b = orders[a][stage]
            waiting[a] = []
            for r in held[a]:
                place = flip(dp, r)
                waiting[a].append(s.start(buf.at[place], buf.at[place], "dp", flip(dp, b)))
            held[a] = held[a] + [r ^ b for r in held[a]]
    for copy in waiting[0] + waiting[1] + late:
        copy.wait_recv()
    s.drain()


def dispatch(n, parts, x, c, t, up, down, dec):
    half = n // 2
    stack = lambda v: jax.ShapeDtypeStruct((half - 1,) + v.shape, v.dtype)
    same = lambda v: jax.ShapeDtypeStruct(v.shape, v.dtype)
    copies = 3 + 3 * (half - 1) + 2 * (parts - 1)
    anywhere = pl.BlockSpec(memory_space=pl.ANY)
    return pl.pallas_call(
        partial(dispatch_kernel, n, parts),
        out_shape=(stack(x), stack(c), stack(t), same(up), same(down), same(dec)),
        in_specs=[anywhere] * 6,
        out_specs=[anywhere] * 6,
        scratch_shapes=[pltpu.SemaphoreType.DMA((copies,)), pltpu.SemaphoreType.DMA((copies,))],
        compiler_params=pltpu.CompilerParams(collective_id=0, has_side_effects=True),
        name="dispatch",
    )(x, c, t, up, down, dec)


def add_rows(rows, read_a, read_b, write):
    step = 32 if rows % 32 == 0 else rows

    @pl.loop(0, rows // step)
    def _(i):
        cut = pl.ds(pl.multiple_of(i * step, step), step)
        write(cut, read_a(cut).astype(F32) + read_b(cut).astype(F32))


def return_kernel(n, parts, up1, down1, up2, down2, lay, bak, dots, upo, downo, layo, bako, dotso,
                  slots, far, send, recv):
    ex, dp = greet(n, parts)
    half = n // 2
    s = Sender(send, recv)
    rows = up1.shape[1]
    grads = (up1, down1, up2, down2)
    orders = bit_orders(parts)
    orders = (orders[0], orders[1], orders[0], orders[1])
    stages = len(orders[0])
    place, keep = [], []
    for a in range(4):
        ids, kept, live, k = {}, [], list(range(parts)), 0
        for st in range(stages):
            live = [r for r in live if not r & orders[a][st]]
            kept.append(live)
            for r in live:
                ids[(st, r)] = k
                k += 1
        place.append(ids)
        keep.append(kept)

    def begin(a, st):
        b = orders[a][st]
        out = []
        for r in keep[a][st]:
            far_r = r ^ b
            src = grads[a].at[flip(dp, far_r)] if st == 0 else slots.at[a, place[a][(st - 1, far_r)]]
            out.append(s.start(src, slots.at[a, place[a][(st, r)]], "dp", flip(dp, b)))
        return out

    def finish(a, st, copies):
        for copy in copies:
            copy.wait_recv()
        for r in keep[a][st]:
            k = place[a][(st, r)]
            if st == 0:
                chunk = flip(dp, r)
                other = lambda cut: grads[a][chunk, cut, :]
            else:
                old = place[a][(st - 1, r)]
                other = lambda cut: slots[a, old, cut, :]
            if st == stages - 1 and a < 2:
                out = (upo, downo)[a]
                def write(cut, v):
                    out[cut, :] = v
            else:
                def write(cut, v):
                    slots[a, k, cut, :] = v.astype(BF)
            add_rows(rows, lambda cut: slots[a, k, cut, :], other, write)

    late = []
    run = {}
    for a in (2, 3, 0, 1):
        run[a] = begin(a, 0)
    for d in range(1, half):
        to_dev = flip(ex, d)
        late.append(s.start(lay.at[d - 1], layo.at[d - 1], "expert", to_dev))
        late.append(s.start(bak.at[d - 1], bako.at[d - 1], "expert", to_dev))
        late.append(s.start(dots.at[d - 1], dotso.at[d - 1], "expert", to_dev))
    swaps = []
    for st in range(stages):
        for a in (2, 3):
            finish(a, st, run[a])
            if st + 1 < stages:
                run[a] = begin(a, st + 1)
            else:
                k = place[a][(st, 0)]
                swaps.append(s.start(slots.at[a, k], far.at[a - 2], "expert", flip(ex, half)))
        if st > 0:
            for a in (0, 1):
                finish(a, st - 1, run[a])
                run[a] = begin(a, st)
    for a in (0, 1):
        finish(a, stages - 1, run[a])
    for a, out in ((0, upo), (1, downo)):
        swaps[a].wait_recv()

        def write(cut, v, out=out):
            out[cut, :] = v

        add_rows(rows, lambda cut: out[cut, :], lambda cut: far[a, cut, :], write)
    for copy in late:
        copy.wait_recv()
    s.drain()


def give_back(n, parts, grads, lay, bak, dots):
    half = n // 2
    same = lambda v: jax.ShapeDtypeStruct(v.shape, v.dtype)
    rows, cols = grads[0].shape[1:]
    copies = 4 * (parts - 1) + 2 + 3 * (half - 1)
    anywhere = pl.BlockSpec(memory_space=pl.ANY)
    vmem = pl.BlockSpec(memory_space=pltpu.VMEM)
    shard = jax.ShapeDtypeStruct((rows, cols), F32)
    return pl.pallas_call(
        partial(return_kernel, n, parts),
        out_shape=(shard, shard, same(lay), same(bak), same(dots)),
        in_specs=[vmem] * 4 + [anywhere] * 3,
        out_specs=[vmem] * 2 + [anywhere] * 3,
        scratch_shapes=[
            pltpu.VMEM((4, parts - 1, rows, cols), BF),
            pltpu.VMEM((2, rows, cols), BF),
            pltpu.SemaphoreType.DMA((copies,)),
            pltpu.SemaphoreType.DMA((copies,)),
        ],
        compiler_params=pltpu.CompilerParams(
            collective_id=1, has_side_effects=True, vmem_limit_bytes=50 * 2**20
        ),
        name="give_back",
    )(*grads, lay, bak, dots)


def local(tokens, cotangent, routes, gate_probs, w_up, w_down, decay_rate):
    rows, width = tokens.shape
    n = lax.axis_size("expert")
    parts = lax.axis_size("dp")
    half = n // 2
    me = lax.axis_index("expert")
    w_up, w_down, decay = w_up[0], w_down[0], decay_rate[0]
    hidden = w_up.shape[1]
    ids = jnp.arange(n, dtype=jnp.int32)
    hit = routes[None, :, :] == ids[:, None, None]
    table = jnp.sum(jnp.where(hit, gate_probs[None, :, :], 0.0), axis=2)
    x_far, cot_far, tab_far, w_up2, w_down2, decay2 = dispatch(
        n, parts, tokens, cotangent, table,
        w_up.reshape(parts, width // parts, hidden),
        w_down.reshape(parts, hidden // parts, width),
        decay[None],
    )
    w_up2 = w_up2.reshape(width, hidden)
    w_down2 = w_down2.reshape(hidden, width)
    decay2 = decay2[0]
    x_all = jnp.concatenate([tokens, x_far.reshape(-1, width)], axis=0)
    cot_all = jnp.concatenate([cotangent, cot_far.reshape(-1, width)], axis=0)
    tabs = jnp.concatenate([table[None], tab_far], axis=0)
    other = me ^ half

    def gate_of(expert):
        pick = (ids == expert)[None, :, None]
        return jnp.sum(jnp.where(pick, tabs, 0.0), axis=1).reshape(-1)

    def grad(a, b):
        return mm(a, b, ((0,), (0,))).astype(BF).reshape(parts, width // parts, hidden)

    layer1, dots1, back1, rates1, scaled1, cg1 = expert_block(
        x_all, cot_all, gate_of(me), w_up, w_down, decay
    )
    layer2, dots2, back2, rates2, scaled2, cg2 = expert_block(
        x_all, cot_all, gate_of(other), w_up2, w_down2, decay2
    )
    grads = (grad(x_all, cg1), grad(scaled1, rates1), grad(x_all, cg2), grad(scaled2, rates2))
    layer = (layer1 + layer2).reshape(half, rows, width)
    back = (back1 + back2).reshape(half, rows, width)
    dots = jnp.where((ids == me)[None, :, None], dots1.reshape(half, 1, rows), 0.0) + jnp.where(
        (ids == other)[None, :, None], dots2.reshape(half, 1, rows), 0.0
    )
    up_grad, down_grad, layer_far, back_far, dots_far = give_back(
        n, parts, grads, layer[1:].astype(BF), back[1:].astype(BF), dots[1:]
    )
    layer_out = layer[0] + jnp.sum(layer_far.astype(F32), axis=0)
    token_grad = back[0] + jnp.sum(back_far.astype(F32), axis=0)
    own = dots[0] + jnp.sum(dots_far, axis=0)
    gate_grad = jnp.sum(jnp.where(hit, own[:, :, None], 0.0), axis=0)
    return (layer_out.astype(BF), token_grad.astype(BF), gate_grad, up_grad[None], down_grad.T[None])


def solution(mesh):
    rows = P(("dp", "expert"), None)
    return jax.shard_map(
        local,
        mesh=mesh,
        in_specs=(rows, rows, rows, rows, P("expert", None, None), P("expert", None, None), P("expert", None)),
        out_specs=(rows, rows, rows, P("expert", "dp", None), P("expert", None, "dp")),
        check_vma=False,
    )
```

profile of v0, /device:TPU:0, one launch (start us, length us, event | category | flops | bytes accessed | tf_op | source)
XLA Modules:
  0.0 213.4 jit_solution(8779687755132107277)
XLA Ops:
  0.6 0.7 reduce
  1.4 1.3 select_reduce_fusion.3.t
  2.7 73.1 %dispatch.1 = (bf16[1,256,2048]{2,1,0:T(8,128)(2,1)}, bf16[1,256,2048]{2,1,0:T(8,128)(2,1)}, f32[1,4,256]{2,1,0:T(4,128)}, bf16[8,256,768]{2,1,0:T(8,128)(2,1)},...) custom-call(bf16[256,2048]{1,0:T(8,128)(2,1)} %x.1, bf16[256,2048]{1,0:T(8,128)(2,1)} %c.1, ...), custom_call_target="tpu_custom_call" | custom-call | tf_op jit(solution)/shard_map/dispatch/pallas_call | solution.py:137
  75.8 0.8 select_reduce_fusion.2
  76.6 0.7 reduce.1
  77.3 0.0 copy-start.5
  77.3 5.9 %multiply_convert_fusion.2 = (bf16[512,768]{1,0:T(8,128)(2,1)S(1)}, f32[512,768]{1,0:T(8,128)S(1)}) fusion(f32[768]{0:T(1024)S(1)} %reduce.1, f32[768]{0:T(1024)S(1)} %get-tuple-element.43, bf16[2048,768]{1,0:T(8,128)(2,1)} %bitcast.80, bf16[256,2048]{1,0:T(8,128)(2,1)} %bitcast.84, bf16[256,2048]{1,0:T(8,128)(2,1)S(1)} %copy-done.6), kind=kOutput, calls=%fused_computation.38 | convolution fusion | flops 1628569600 | bytes 7608320 | tf_op jit(solution)/shard_map/dot_general | solution.py:35
  83.3 6.2 %multiply_convert_fusion = bf16[512,768]{1,0:T(8,128)(2,1)S(1)} fusion(bf16[768,2048]{1,0:T(8,128)(2,1)S(1)} %bitcast.82, f32[512]{0:T(512)S(1)} %bitcast.77, f32[768]{0:T(1024)S(1)} %get-tuple-element.42, f32[768]{0:T(1024)S(1)} %reduce.1, f32[512,768]{1,0:T(8,128)S(1)} %get-tuple-element.49, f32[768]{0:T(1024)S(1)} %get-tuple-element.43, ...), kind=kOutput, calls=%fused_computation.36 | convolution fusion | flops 1640890368 | bytes 7613440 | tf_op jit(solution)/shard_map/dot_general | solution.py:35
  89.5 1.8 convolution_convert_fusion.5
  91.4 0.0 copy-start
  91.4 3.7 %convolution_convert_fusion = bf16[2048,768]{1,0:T(8,128)(2,1)} fusion(bf16[512,768]{1,0:T(8,128)(2,1)S(1)} %get-tuple-element.48, f32[512]{0:T(512)S(1)} %bitcast.78, bf16[256,2048]{1,0:T(8,128)(2,1)S(1)} %bitcast.89, bf16[256,2048]{1,0:T(8,128)(2,1)S(1)} %copy-done.5), kind=kOutput, calls=%fused_computation.12 | convolution fusion | flops 1618477056 | bytes 6031360 | tf_op jit(solution)/shard_map/dot_general | solution.py:35
  95.1 3.6 %multiply_convert_fusion.3 = (bf16[512,768]{1,0:T(8,128)(2,1)S(1)}, f32[512,768]{1,0:T(8,128)S(1)}) fusion(f32[768]{0:T(1024)S(1)} %reduce, f32[768]{0:T(1024)S(1)} %get-tuple-element.45, bf16[1,2048,768]{2,1,0:T(8,128)(2,1)S(1)} %copy-done, bf16[256,2048]{1,0:T(8,128)(2,1)S(1)} %bitcast.85, bf16[256,2048]{1,0:T(8,128)(2,1)S(1)} %copy-done.6), kind=kOutput, calls=%fused_computation.45 | convolution fusion | flops 1628569600 | bytes 7608320 | tf_op jit(solution)/shard_map/dot_general | solution.py:35
  98.7 0.0 copy-start.16
  98.7 6.3 %multiply_convert_fusion.1 = bf16[512,768]{1,0:T(8,128)(2,1)S(1)} fusion(bf16[1,768,2048]{2,1,0:T(8,128)(2,1)S(1)} %copy-done.1, f32[512]{0:T(512)S(1)} %bitcast.74, f32[768]{0:T(1024)S(1)} %get-tuple-element.44, f32[768]{0:T(1024)S(1)} %reduce, f32[512,768]{1,0:T(8,128)S(1)} %get-tuple-element.47, f32[768]{0:T(1024)S(1)} %get-tuple-element.45, ...), kind=kOutput, calls=%fused_computation.37 | convolution fusion | flops 1640890368 | bytes 7613440 | tf_op jit(solution)/shard_map/dot_general | solution.py:35
  105.0 0.9 copy-done.18
  105.9 1.8 fusion.13
  107.7 0.0 copy-done.9
  107.8 1.8 convert_add_fusion
  109.6 1.2 fusion.24.bak
  110.9 4.6 %fusion.3 = (f32[512]{0:T(512)S(1)}, f32[512]{0:T(512)S(1)}, f32[512,2048]{1,0:T(8,128)}) fusion(bf16[256,2048]{1,0:T(8,128)(2,1)S(1)} %bitcast.91, bf16[256,2048]{1,0:T(8,128)(2,1)S(1)} %copy-done.5, bf16[512,2048]{1,0:T(8,128)(2,1)S(1)} %convolution_convert_fusion.5, f32[512]{0:T(512)S(1)} %bitcast.79, f32[512]{0:T(512)S(1)} %bitcast.75, ...), kind=kOutput, calls=%fused_computation.9 | convolution fusion | flops 1625291776 | bytes 12328960 | tf_op jit(solution)/shard_map/dot_general | solution.py:35
  115.5 0.1 select_add_fusion
  115.6 2.8 %fusion.23.lay = bf16[1,256,2048]{2,1,0:T(8,128)(2,1)} fusion(f32[512,2048]{1,0:T(8,128)} %get-tuple-element.41), kind=kLoop, calls=%fused_computation.52 | loop fusion | bytes 2097152 | tf_op jit(solution)/shard_map/convert_element_type | solution.py:315
  118.5 3.7 %convolution_convert_fusion.2 = bf16[2048,768]{1,0:T(8,128)(2,1)} fusion(bf16[512,768]{1,0:T(8,128)(2,1)S(1)} %copy-done.17, f32[512]{0:T(512)S(1)} %bitcast.76, bf16[256,2048]{1,0:T(8,128)(2,1)S(1)} %bitcast.92, bf16[256,2048]{1,0:T(8,128)(2,1)S(1)} %copy-done.5), kind=kOutput, calls=%fused_computation.14 | convolution fusion | flops 1618477056 | bytes 6031360 | tf_op jit(solution)/shard_map/dot_general | solution.py:35
  122.2 3.5 %convolution_convert_fusion.1 = bf16[2048,768]{1,0:T(8,128)(2,1)} fusion(bf16[512,768]{1,0:T(8,128)(2,1)S(1)} %copy-done.15, bf16[256,2048]{1,0:T(8,128)(2,1)S(1)} %bitcast.86, bf16[256,2048]{1,0:T(8,128)(2,1)S(1)} %copy-done.6), kind=kOutput, calls=%fused_computation.13 | convolution fusion | flops 1616379904 | bytes 6029312 | tf_op jit(solution)/shard_map/dot_general | solution.py:35
  125.7 3.5 %convolution_convert_fusion.3 = bf16[2048,768]{1,0:T(8,128)(2,1)} fusion(bf16[512,768]{1,0:T(8,128)(2,1)S(1)} %copy-done.19, bf16[256,2048]{1,0:T(8,128)(2,1)S(1)} %bitcast.87, bf16[256,2048]{1,0:T(8,128)(2,1)S(1)} %copy-done.6), kind=kOutput, calls=%fused_computation.15 | convolution fusion | flops 1616379904 | bytes 6029312 | tf_op jit(solution)/shard_map/dot_general | solution.py:35
  129.2 77.7 %give_back.1 = (f32[256,768]{1,0:T(8,128)S(1)}, f32[256,768]{1,0:T(8,128)S(1)}, bf16[1,256,2048]{2,1,0:T(8,128)(2,1)S(1)}, bf16[1,256,2048]{2,1,0:T(8,128)(2,1)S(1)}, f32[1,4,256]{2,1,0:T(4,128)S(1)}) custom-call(bf16[8,256,768]{2,1,0:T(8,128)(2,1)} %bitcast.70, bf16[8,256,768]{2,1,0:T(8,128)(2,1)} %bitcast.68, bf16[8,256,768]{2,1,0:T(8,128)(2,1)} %bitcast.69, ...), custom_call_target="tpu_custom_call" | custom-call | tf_op jit(solution)/shard_map/give_back/pallas_call | solution.py:252
  207.0 0.6 select_reduce_fusion
  207.6 1.3 fusion.19
  208.8 1.3 copy-done.4
  210.1 1.3 fusion.20
  211.4 1.1 copy.15
  212.5 0.9 copy.19
  (43 shorter events, 0.1 us)
Async XLA Ops:
  2.7 73.1 %copy-start.7 = (f32[4,256]{1,0:T(4,128)S(1)}, f32[4,256]{1,0:T(4,128)}, u32[]{:S(2)}) copy-start(f32[4,256]{1,0:T(4,128)} %select_reduce_fusion.3.t) | copy-start | bytes 12292
  2.7 74.6 %copy-start.6 = (bf16[256,2048]{1,0:T(8,128)(2,1)S(1)}, bf16[256,2048]{1,0:T(8,128)(2,1)}, u32[]{:S(2)}) copy-start(bf16[256,2048]{1,0:T(8,128)(2,1)} %x.1) | copy-start | bytes 3145732
  77.3 6.0 %copy-start.5 = (bf16[256,2048]{1,0:T(8,128)(2,1)S(1)}, bf16[256,2048]{1,0:T(8,128)(2,1)}, u32[]{:S(2)}) copy-start(bf16[256,2048]{1,0:T(8,128)(2,1)} %c.1) | copy-start | bytes 3145732
  77.3 6.0 %copy-start.10 = (bf16[8,96,2048]{2,1,0:T(8,128)(2,1)S(1)}, bf16[8,96,2048]{2,1,0:T(8,128)(2,1)}, u32[]{:S(2)}) copy-start(bf16[8,96,2048]{2,1,0:T(8,128)(2,1)} %get-tuple-element.20) | copy-start | bytes 9437188
  77.3 6.0 %copy-start.12 = (bf16[1,256,2048]{2,1,0:T(8,128)(2,1)S(1)}, bf16[1,256,2048]{2,1,0:T(8,128)(2,1)}, u32[]{:S(2)}) copy-start(bf16[1,256,2048]{2,1,0:T(8,128)(2,1)} %get-tuple-element.21) | copy-start | bytes 3145732
  89.5 18.2 %copy-start.14 = (bf16[512,768]{1,0:T(8,128)(2,1)}, bf16[512,768]{1,0:T(8,128)(2,1)S(1)}, u32[]{:S(2)}) copy-start(bf16[512,768]{1,0:T(8,128)(2,1)S(1)} %multiply_convert_fusion) | copy-start | bytes 2359300
  91.4 3.7 %copy-start = (bf16[1,2048,768]{2,1,0:T(8,128)(2,1)S(1)}, bf16[1,2048,768]{2,1,0:T(8,128)(2,1)}, u32[]{:S(2)}) copy-start(bf16[1,2048,768]{2,1,0:T(8,128)(2,1)} %param.11) | copy-start | bytes 9437188
  91.4 3.7 %copy-start.11 = (bf16[1,256,2048]{2,1,0:T(8,128)(2,1)S(1)}, bf16[1,256,2048]{2,1,0:T(8,128)(2,1)}, u32[]{:S(2)}) copy-start(bf16[1,256,2048]{2,1,0:T(8,128)(2,1)} %get-tuple-element.17) | copy-start | bytes 3145732
  95.1 3.6 %copy-start.1 = (bf16[1,768,2048]{2,1,0:T(8,128)(2,1)S(1)}, bf16[1,768,2048]{2,1,0:T(8,128)(2,1)}, u32[]{:S(2)}) copy-start(bf16[1,768,2048]{2,1,0:T(8,128)(2,1)} %param.12) | copy-start | bytes 9437188
  98.7 12.2 %copy-start.16 = (bf16[512,768]{1,0:T(8,128)(2,1)}, bf16[512,768]{1,0:T(8,128)(2,1)S(1)}, u32[]{:S(2)}) copy-start(bf16[512,768]{1,0:T(8,128)(2,1)S(1)} %get-tuple-element.46) | copy-start | bytes 2359300
  105.0 0.9 copy-start.18
  105.9 1.9 copy-start.9
  109.6 5.9 %copy-start.2 = (f32[512,2048]{1,0:T(8,128)}, f32[512,2048]{1,0:T(8,128)S(1)}, u32[]{:S(2)}) copy-start(f32[512,2048]{1,0:T(8,128)S(1)} %convert_add_fusion) | copy-start | bytes 12582916
  115.5 2.9 %copy-start.13 = (bf16[1,256,2048]{2,1,0:T(8,128)(2,1)S(1)}, bf16[1,256,2048]{2,1,0:T(8,128)(2,1)}, u32[]{:S(2)}) copy-start(bf16[1,256,2048]{2,1,0:T(8,128)(2,1)} %get-tuple-element.21) | copy-start | bytes 3145732
  115.5 2.9 %copy-start.17 = (bf16[512,768]{1,0:T(8,128)(2,1)S(1)}, bf16[512,768]{1,0:T(8,128)(2,1)}, u32[]{:S(2)}) copy-start(bf16[512,768]{1,0:T(8,128)(2,1)} %copy-done.16) | copy-start | bytes 2359300
  118.5 3.7 %copy-start.15 = (bf16[512,768]{1,0:T(8,128)(2,1)S(1)}, bf16[512,768]{1,0:T(8,128)(2,1)}, u32[]{:S(2)}) copy-start(bf16[512,768]{1,0:T(8,128)(2,1)} %copy-done.14) | copy-start | bytes 2359300
  122.2 3.5 %copy-start.19 = (bf16[512,768]{1,0:T(8,128)(2,1)S(1)}, bf16[512,768]{1,0:T(8,128)(2,1)}, u32[]{:S(2)}) copy-start(bf16[512,768]{1,0:T(8,128)(2,1)} %copy-done.18) | copy-start | bytes 2359300
  129.2 77.8 %copy-start.8 = (s32[256,2]{0,1:T(2,128)S(1)}, s32[256,2]{0,1:T(2,128)}, u32[]{:S(2)}) copy-start(s32[256,2]{0,1:T(2,128)} %param.9) | copy-start | bytes 6148
  129.2 78.4 %copy-start.3 = (f32[512,2048]{1,0:T(8,128)S(1)}, f32[512,2048]{1,0:T(8,128)}, u32[]{:S(2)}) copy-start(f32[512,2048]{1,0:T(8,128)} %copy-done.2) | copy-start | bytes 12582916
  207.6 2.6 %copy-start.4 = (f32[512,2048]{1,0:T(8,128)S(1)}, f32[512,2048]{1,0:T(8,128)}, u32[]{:S(2)}) copy-start(f32[512,2048]{1,0:T(8,128)} %get-tuple-element.41) | copy-start | bytes 12582916
where the time goes:
time: 214 us; the launch traced here: 213 us
  Pallas kernels  151 us (71%)
  matrix products  46.5 us (22%)
  local copies, waits for them, and re-layouts  8.43 us (4%)
  other arithmetic  6.68 us (3%)
    pallas_call x1, Pallas kernels, give_back(): pl.pallas_call(partial(return_kernel, n, parts), out_shape=(shard, shard,...  77.7 us
    pallas_call x1, Pallas kernels, dispatch(): pl.pallas_call(partial(dispatch_kernel, n, parts), out_shape=(stack(x), s...  73.1 us
    dot_general x12, matrix products, mm(): return lax.dot_general(a, b, (dims, ((), ())), preferred_element_type=F32)  46.5 us
    unnamed x44, local copies, waits for them, and re-layouts  4.34 us

commit v1 on v0

--- a/solution.py
+++ b/solution.py
@@ -154,13 +154,27 @@
         write(cut, read_a(cut).astype(F32) + read_b(cut).astype(F32))
 
 
-def return_kernel(n, parts, up1, down1, up2, down2, lay, bak, dots, upo, downo, layo, bako, dotso,
-                  slots, far, send, recv):
+def return_kernel(n, parts, x, cg1, sc1, rt1, cg2, sc2, rt2, lay, bak, dots, upo, downo, layo, bako,
+                  dotso, products, slots, far, send, recv):
     ex, dp = greet(n, parts)
     half = n // 2
     s = Sender(send, recv)
-    rows = up1.shape[1]
-    grads = (up1, down1, up2, down2)
+    rows = slots.shape[2]
+    grads = [products.at[a] for a in range(4)]
+    pairs = ((x, cg1), (sc1, rt1), (x, cg2), (sc2, rt2))
+    tile = 256
+    per = tile // rows
+
+    def multiply(a):
+        left, right = pairs[a]
+
+        @pl.loop(0, left.shape[1] // tile)
+        def _(i):
+            cols = pl.ds(pl.multiple_of(i * tile, tile), tile)
+            res = mm(left[:, cols], right[...], ((0,), (0,))).astype(BF)
+            for k in range(per):
+                products[a, i * per + k] = res[k * rows:(k + 1) * rows]
+
     orders = bit_orders(parts)
     orders = (orders[0], orders[1], orders[0], orders[1])
     stages = len(orders[0])
@@ -192,7 +206,7 @@
             k = place[a][(st, r)]
             if st == 0:
                 chunk = flip(dp, r)
-                other = lambda cut: grads[a][chunk, cut, :]
+                other = lambda cut: products[a, chunk, cut, :]
             else:
                 old = place[a][(st - 1, r)]
                 other = lambda cut: slots[a, old, cut, :]
@@ -207,13 +221,14 @@
 
     late = []
     run = {}
-    for a in (2, 3, 0, 1):
-        run[a] = begin(a, 0)
     for d in range(1, half):
         to_dev = flip(ex, d)
         late.append(s.start(lay.at[d - 1], layo.at[d - 1], "expert", to_dev))
         late.append(s.start(bak.at[d - 1], bako.at[d - 1], "expert", to_dev))
         late.append(s.start(dots.at[d - 1], dotso.at[d - 1], "expert", to_dev))
+    for a in (2, 3):
+        multiply(a)
+        run[a] = begin(a, 0)
     swaps = []
     for st in range(stages):
         for a in (2, 3):
@@ -223,8 +238,11 @@
             else:
                 k = place[a][(st, 0)]
                 swaps.append(s.start(slots.at[a, k], far.at[a - 2], "expert", flip(ex, half)))
-        if st > 0:
-            for a in (0, 1):
+        for a in (0, 1):
+            if st == 0:
+                multiply(a)
+                run[a] = begin(a, 0)
+            else:
                 finish(a, st - 1, run[a])
                 run[a] = begin(a, st)
     for a in (0, 1):
@@ -241,10 +259,10 @@
     s.drain()
 
 
-def give_back(n, parts, grads, lay, bak, dots):
+def give_back(n, parts, factors, lay, bak, dots):
     half = n // 2
     same = lambda v: jax.ShapeDtypeStruct(v.shape, v.dtype)
-    rows, cols = grads[0].shape[1:]
+    rows, cols = factors[0].shape[1] // parts, factors[1].shape[1]
     copies = 4 * (parts - 1) + 2 + 3 * (half - 1)
     anywhere = pl.BlockSpec(memory_space=pl.ANY)
     vmem = pl.BlockSpec(memory_space=pltpu.VMEM)
@@ -252,9 +270,10 @@
     return pl.pallas_call(
         partial(return_kernel, n, parts),
         out_shape=(shard, shard, same(lay), same(bak), same(dots)),
-        in_specs=[vmem] * 4 + [anywhere] * 3,
+        in_specs=[vmem] * 7 + [anywhere] * 3,
         out_specs=[vmem] * 2 + [anywhere] * 3,
         scratch_shapes=[
+            pltpu.VMEM((4, parts, rows, cols), BF),
             pltpu.VMEM((4, parts - 1, rows, cols), BF),
             pltpu.VMEM((2, rows, cols), BF),
             pltpu.SemaphoreType.DMA((copies,)),
@@ -264,7 +283,7 @@
             collective_id=1, has_side_effects=True, vmem_limit_bytes=50 * 2**20
         ),
         name="give_back",
-    )(*grads, lay, bak, dots)
+    )(*factors, lay, bak, dots)
 
 
 def local(tokens, cotangent, routes, gate_probs, w_up, w_down, decay_rate):
@@ -296,23 +315,20 @@
         pick = (ids == expert)[None, :, None]
         return jnp.sum(jnp.where(pick, tabs, 0.0), axis=1).reshape(-1)
 
-    def grad(a, b):
-        return mm(a, b, ((0,), (0,))).astype(BF).reshape(parts, width // parts, hidden)
-
     layer1, dots1, back1, rates1, scaled1, cg1 = expert_block(
         x_all, cot_all, gate_of(me), w_up, w_down, decay
     )
     layer2, dots2, back2, rates2, scaled2, cg2 = expert_block(
         x_all, cot_all, gate_of(other), w_up2, w_down2, decay2
     )
-    grads = (grad(x_all, cg1), grad(scaled1, rates1), grad(x_all, cg2), grad(scaled2, rates2))
+    factors = (x_all, cg1, scaled1, rates1, cg2, scaled2, rates2)
     layer = (layer1 + layer2).reshape(half, rows, width)
     back = (back1 + back2).reshape(half, rows, width)
     dots = jnp.where((ids == me)[None, :, None], dots1.reshape(half, 1, rows), 0.0) + jnp.where(
         (ids == other)[None, :, None], dots2.reshape(half, 1, rows), 0.0
     )
     up_grad, down_grad, layer_far, back_far, dots_far = give_back(
-        n, parts, grads, layer[1:].astype(BF), back[1:].astype(BF), dots[1:]
+        n, parts, factors, layer[1:].astype(BF), back[1:].astype(BF), dots[1:]
     )
     layer_out = layer[0] + jnp.sum(layer_far.astype(F32), axis=0)
     token_grad = back[0] + jnp.sum(back_far.astype(F32), axis=0)

time: 214 us -> 211 us (0.986)
  matrix products: 46.5 us -> 41.7 us
  Pallas kernels: 151 us -> 154 us
  local copies, waits for them, and re-layouts: 8.43 us -> 5.94 us
    dot_general x12 -> x8, matrix products: 46.5 us -> 41.7 us  [mm(): return lax.dot_general(a, b, (dims, ((), ())), preferred_element_type=F32)]
    pallas_call x1, Pallas kernels: 77.7 us -> 80.8 us  [give_back(): pl.pallas_call(partial(return_kernel, n, parts), out_shape=(shard, shard,...]
    unnamed x44 -> x36, local copies, waits for them, and re-layouts: 4.34 us -> 3.68 us
where the time goes in v1:
time: 211 us
  Pallas kernels  154 us (73%)
  matrix products  41.7 us (20%)
  other arithmetic  8.27 us (4%)
  local copies, waits for them, and re-layouts  5.94 us (3%)
    pallas_call x1, Pallas kernels, give_back(): pl.pallas_call(partial(return_kernel, n, parts), out_shape=(shard, shard,...  80.8 us
    pallas_call x1, Pallas kernels, dispatch(): pl.pallas_call(partial(dispatch_kernel, n, parts), out_shape=(stack(x), s...  73.1 us
    dot_general x8, matrix products, mm(): return lax.dot_general(a, b, (dims, ((), ())), preferred_element_type=F32)  41.7 us

profile of v1, /device:TPU:0, one launch (start us, length us, event | category | flops | bytes accessed | tf_op | source)
XLA Modules:
  0.0 210.7 jit_solution(17247321587804929472)
XLA Ops:
  0.6 1.3 select_reduce_fusion.3.t
  1.9 73.1 %dispatch.1 = (bf16[1,256,2048]{2,1,0:T(8,128)(2,1)}, bf16[1,256,2048]{2,1,0:T(8,128)(2,1)}, f32[1,4,256]{2,1,0:T(4,128)}, bf16[8,256,768]{2,1,0:T(8,128)(2,1)},...) custom-call(bf16[256,2048]{1,0:T(8,128)(2,1)} %x.1, bf16[256,2048]{1,0:T(8,128)(2,1)} %c.1, ...), custom_call_target="tpu_custom_call" | custom-call | tf_op jit(solution)/shard_map/dispatch/pallas_call | solution.py:137
  75.1 0.7 reduce.1
  75.8 0.0 copy-done
  75.8 0.0 copy-start.13
  75.8 6.9 %multiply_convert_fusion.2 = (bf16[512,768]{1,0:T(8,128)(2,1)S(1)}, f32[512,768]{1,0:T(8,128)}) fusion(f32[768]{0:T(1024)S(1)} %reduce.1, f32[768]{0:T(1024)S(1)} %get-tuple-element.45, bf16[2048,768]{1,0:T(8,128)(2,1)} %bitcast.69, bf16[256,2048]{1,0:T(8,128)(2,1)} %bitcast.61, bf16[256,2048]{1,0:T(8,128)(2,1)S(1)} %copy-done), kind=kOutput, calls=%fused_computation.34 | convolution fusion | flops 1628569600 | bytes 7608320 | tf_op jit(solution)/shard_map/dot_general | solution.py:35
  82.7 0.0 copy-done.13
  82.7 3.2 %convolution_convert_fusion.1 = bf16[512,2048]{1,0:T(8,128)(2,1)} fusion(bf16[512,768]{1,0:T(8,128)(2,1)S(1)} %get-tuple-element.50.rt2, bf16[768,2048]{1,0:T(8,128)(2,1)S(1)} %bitcast.71), kind=kOutput, calls=%fused_computation.23 | convolution fusion | flops 1611661312 | bytes 6029312 | tf_op jit(solution)/shard_map/dot_general | solution.py:35
  85.9 0.0 copy-done.7
  85.9 0.0 copy-start.8
  86.0 0.0 copy-start.4
  86.0 6.8 %multiply_convert_fusion.3 = (bf16[512,768]{1,0:T(8,128)(2,1)S(1)}, f32[512,768]{1,0:T(8,128)}) fusion(f32[768]{0:T(1024)S(1)} %reduce, f32[768]{0:T(1024)S(1)} %get-tuple-element.47, bf16[1,2048,768]{2,1,0:T(8,128)(2,1)} %param.11, bf16[256,2048]{1,0:T(8,128)(2,1)} %bitcast.62, bf16[256,2048]{1,0:T(8,128)(2,1)S(1)} %copy-done), kind=kOutput, calls=%fused_computation.41 | convolution fusion | flops 1628569600 | bytes 7608320 | tf_op jit(solution)/shard_map/dot_general | solution.py:35
  92.8 0.1 select_reduce_fusion.2
  93.0 7.9 %fusion.3 = (f32[512]{0:T(512)S(1)}, f32[512]{0:T(512)S(1)}, f32[512,2048]{1,0:T(8,128)}, bf16[512,2048]{1,0:T(8,128)(2,1)}, bf16[512,2048]{1,0:T(8,128)(2,1)}) fusion(bf16[256,2048]{1,0:T(8,128)(2,1)} %bitcast.73, bf16[256,2048]{1,0:T(8,128)(2,1)S(1)} %copy-done.4, bf16[512,2048]{1,0:T(8,128)(2,1)} %convolution_convert_fusion.1, f32[512]{0:T(512)S(1)} %bitcast.68, ...), kind=kOutput, calls=%fused_computation.9 | convolution fusion | flops 1629486080 | bytes 16523264 | tf_op jit(solution)/shard_map/dot_general | solution.py:35
  100.9 0.1 select_add_fusion
  101.0 8.0 %multiply_convert_fusion.1.cg1 = bf16[512,768]{1,0:T(8,128)(2,1)S(1)} fusion(bf16[512,2048]{1,0:T(8,128)(2,1)} %get-tuple-element.43.sc1, bf16[1,768,2048]{2,1,0:T(8,128)(2,1)} %param.12, f32[768]{0:T(1024)S(1)} %get-tuple-element.46, f32[768]{0:T(1024)S(1)} %reduce, f32[512,768]{1,0:T(8,128)} %get-tuple-element.49, f32[768]{0:T(1024)S(1)} %get-tuple-element.47), kind=kOutput, calls=%fused_computation.33 | convolution fusion | flops 1634598912 | bytes 7611392 | tf_op jit(solution)/shard_map/dot_general | solution.py:35
  109.1 1.8 fusion.13
  110.9 0.0 copy-done.3
  110.9 0.6 copy-done.14
  111.6 0.5 copy-done.15
  112.0 5.1 %multiply_convert_fusion.cg2 = bf16[512,768]{1,0:T(8,128)(2,1)S(1)} fusion(bf16[512,2048]{1,0:T(8,128)(2,1)S(1)} %copy-done.3, bf16[768,2048]{1,0:T(8,128)(2,1)S(1)} %bitcast.72, f32[768]{0:T(1024)S(1)} %get-tuple-element.44, f32[768]{0:T(1024)S(1)} %reduce.1, f32[512,768]{1,0:T(8,128)S(1)} %copy-done.15, f32[768]{0:T(1024)S(1)} %get-tuple-element.45), kind=kOutput, calls=%fused_computation.32 | convolution fusion | flops 1634598912 | bytes 7611392 | tf_op jit(solution)/shard_map/dot_general | solution.py:35
  117.2 1.9 convert_add_fusion
  119.1 1.1 fusion.24.bak
  120.2 1.1 fusion.23.lay
  121.3 0.5 copy-done.5
  121.8 1.6 pad_maximum_fusion.x
  123.4 80.8 %give_back.1 = (f32[256,768]{1,0:T(8,128)S(1)}, f32[256,768]{1,0:T(8,128)S(1)}, bf16[1,256,2048]{2,1,0:T(8,128)(2,1)}, bf16[1,256,2048]{2,1,0:T(8,128)(2,1)}, f32[1,4,256]{2,1,0:T(4,128)S(1)}) custom-call(bf16[512,2048]{1,0:T(8,128)(2,1)} %pad_maximum_fusion.x, bf16[512,768]{1,0:T(8,128)(2,1)S(1)} %multiply_convert_fusion.1.cg1, ...), custom_call_target="tpu_custom_call" | custom-call | tf_op jit(solution)/shard_map/give_back/pallas_call | solution.py:270
  204.2 0.6 select_reduce_fusion
  204.8 2.6 %fusion.19 = bf16[256,2048]{1,0:T(8,128)(2,1)} fusion(f32[512,2048]{1,0:T(8,128)S(1)} %convert_add_fusion, bf16[1,256,2048]{2,1,0:T(8,128)(2,1)} %get-tuple-element.23), kind=kLoop, calls=%fused_computation.25 | loop fusion | flops 1572864 | bytes 4194304 | tf_op jit(solution)/shard_map/convert_element_type | solution.py:337
  207.4 1.3 fusion.20
  208.7 1.1 copy.15
  209.8 0.9 copy.19
  (32 shorter events, 0.1 us)
Async XLA Ops:
  1.9 73.9 %copy-start = (bf16[256,2048]{1,0:T(8,128)(2,1)S(1)}, bf16[256,2048]{1,0:T(8,128)(2,1)}, u32[]{:S(2)}) copy-start(bf16[256,2048]{1,0:T(8,128)(2,1)} %x.1) | copy-start | bytes 3145732
  75.8 6.9 %copy-start.13 = (bf16[8,96,2048]{2,1,0:T(8,128)(2,1)S(1)}, bf16[8,96,2048]{2,1,0:T(8,128)(2,1)}, u32[]{:S(2)}) copy-start(bf16[8,96,2048]{2,1,0:T(8,128)(2,1)} %get-tuple-element.20) | copy-start | bytes 9437188
  82.7 3.2 %copy-start.7 = (bf16[512,768]{1,0:T(8,128)(2,1)}, bf16[512,768]{1,0:T(8,128)(2,1)S(1)}, u32[]{:S(2)}) copy-start(bf16[512,768]{1,0:T(8,128)(2,1)S(1)} %get-tuple-element.50.rt2) | copy-start | bytes 2359300
  82.7 3.2 %copy-start.9 = (f32[1,768]{1,0:T(1,128)S(1)}, f32[1,768]{1,0:T(1,128)}, u32[]{:S(2)}) copy-start(f32[1,768]{1,0:T(1,128)} %dec.1) | copy-start | bytes 9220
  85.9 6.9 %copy-start.8 = (f32[4,256]{1,0:T(4,128)S(1)}, f32[4,256]{1,0:T(4,128)}, u32[]{:S(2)}) copy-start(f32[4,256]{1,0:T(4,128)} %select_reduce_fusion.3.t) | copy-start | bytes 12292
  86.0 6.9 %copy-start.11 = (f32[1,4,256]{2,1,0:T(4,128)S(1)}, f32[1,4,256]{2,1,0:T(4,128)}, u32[]{:S(2)}) copy-start(f32[1,4,256]{2,1,0:T(4,128)} %get-tuple-element.16) | copy-start | bytes 12292
  86.0 7.0 %copy-start.4 = (bf16[256,2048]{1,0:T(8,128)(2,1)S(1)}, bf16[256,2048]{1,0:T(8,128)(2,1)}, u32[]{:S(2)}) copy-start(bf16[256,2048]{1,0:T(8,128)(2,1)} %c.1) | copy-start | bytes 3145732
  101.0 8.0 %copy-start.1 = (bf16[1,2048,768]{2,1,0:T(8,128)(2,1)S(1)}, bf16[1,2048,768]{2,1,0:T(8,128)(2,1)}, u32[]{:S(2)}) copy-start(bf16[1,2048,768]{2,1,0:T(8,128)(2,1)} %param.11) | copy-start | bytes 9437188
  109.0 1.9 copy-start.3
  109.0 2.5 %copy-start.14 = (bf16[8,96,2048]{2,1,0:T(8,128)(2,1)S(1)}, bf16[8,96,2048]{2,1,0:T(8,128)(2,1)}, u32[]{:S(2)}) copy-start(bf16[8,96,2048]{2,1,0:T(8,128)(2,1)} %get-tuple-element.20) | copy-start | bytes 9437188
  109.1 3.0 %copy-start.15 = (f32[512,768]{1,0:T(8,128)S(1)}, f32[512,768]{1,0:T(8,128)}, u32[]{:S(2)}) copy-start(f32[512,768]{1,0:T(8,128)} %get-tuple-element.51) | copy-start | bytes 4718596
  112.0 5.2 %copy-start.12 = (bf16[8,256,768]{2,1,0:T(8,128)(2,1)S(1)}, bf16[8,256,768]{2,1,0:T(8,128)(2,1)}, u32[]{:S(2)}) copy-start(bf16[8,256,768]{2,1,0:T(8,128)(2,1)} %get-tuple-element.19) | copy-start | bytes 9437188
  117.2 3.0 %copy-start.2 = (f32[512,2048]{1,0:T(8,128)S(1)}, f32[512,2048]{1,0:T(8,128)}, u32[]{:S(2)}) copy-start(f32[512,2048]{1,0:T(8,128)} %get-tuple-element.41) | copy-start | bytes 12582916
  120.2 1.6 copy-start.5
  123.4 80.8 %copy-start.10 = (s32[256,2]{0,1:T(2,128)S(1)}, s32[256,2]{0,1:T(2,128)}, u32[]{:S(2)}) copy-start(s32[256,2]{0,1:T(2,128)} %param.9) | copy-start | bytes 6148
  204.8 2.6 %copy-start.6 = (bf16[1,256,2048]{2,1,0:T(8,128)(2,1)S(1)}, bf16[1,256,2048]{2,1,0:T(8,128)(2,1)}, u32[]{:S(2)}) copy-start(bf16[1,256,2048]{2,1,0:T(8,128)(2,1)} %get-tuple-element.22) | copy-start | bytes 3145732
